TPU v7x, 32 devices: a whole 2x2x4 slice. The times are simulated.
32 devices in a mesh: clus: 4 (over y, x), trip: 4 (over z), mode: 2 (over core).
Axes of the slice: x: 2, y: 2, z: 4, core: 2. Of those that a mesh axis runs over, the one named last changes fastest.
Arguments:
- force_third: bfloat16 [8, 90, 8100], P('clus', 'mode'), may hold values from -0.0234375 to 0.0234375
- phase_angle: bfloat16 [8, 16], P('clus', 'trip'), may hold values from -3.140625 to 3.140625
- eigenvectors: bfloat16 [32, 90, 180], P('trip'), may hold values from -0.4375 to 0.4375
- frequencies: bfloat16 [32, 90], P('trip'), may hold values from 0.5 to 2
- deviation: bfloat16 [32, 90], P('trip'), may hold values from 0.5 to 2
- send_rows: int32 [4, 32], P('trip'), may hold values from 0 to 7
- trip_table: int32 [16, 3], P('trip'), may hold values from 0 to 31
- irreducible: int32 [16], P('trip'), may hold values from 0 to 3
- multiplicity: int32 [16], P('trip'), may hold values from 1 to 8
- drive_term: float32 [4, 90], P('trip', 'mode'), may hold values from -120 to 120
- boundary: float32 [4, 90], P('trip', 'mode'), may hold values from 5 to 40
Outputs:
- gamma_total: float32 [4, 90], P('trip', 'mode')
- new_deviation: float32 [4, 90], P('trip', 'mode')
All inputs are finite; a program needn't handle non-finite values.
Results may differ from a plain program's by a relative error of at most 0.00095.
Values may be sent and summed in bfloat16 or wider, within the bound.
A program may use at most 64 MiB of HBM per device.

v0:
```python
import functools

import jax
import jax.numpy as jnp
from jax import lax
from jax.experimental import pallas as pl
from jax.experimental.pallas import tpu as pltpu
from jax.sharding import PartitionSpec as P

smearing = 0.3
MESH = pl.DeviceIdType.MESH
LANES = 128
f32 = jnp.float32
bf16 = jnp.bfloat16


def up(value, step):
    return -(-value // step) * step


def pick(index, options):
    chosen = options[0]
    for position in range(1, len(options)):
        chosen = jnp.where(index == position, options[position], chosen)
    return chosen


def kernel(
    dims,
    force_ref,
    tail_ref,
    eig_ref,
    send_rows_ref,
    table_ref,
    irr_ref,
    mult_ref,
    drive_ref,
    bound_ref,
    gamma_ref,
    dev_ref,
    blocks,
    tails,
    wbuf,
    left,
    asked,
    wanted,
    outgoing,
    arrived,
    mine,
    other,
    zbuf,
    zout,
    zin,
    tre,
    tim,
    w0buf,
    ratebuf,
    coupbuf,
    msg,
    inbox,
    f_send,
    f_recv,
    t_send,
    t_recv,
    c_send,
    c_recv,
    e_send,
    e_recv,
    p_send,
    p_recv,
    m_send,
    m_recv,
):
    n_clus, n_trip, n_mode, modes, half, rp, cl, slot, wide = dims
    ep = eig_ref.shape[1]
    flat = force_ref.shape[2]
    unit_rows = cl * rp
    chunks = zbuf.shape[1] // wide
    me_c = lax.axis_index("clus")
    me_t = lax.axis_index("trip")
    me_m = lax.axis_index("mode")
    sib = (me_c, me_t, 1 - me_m)
    odd = lax.rem(me_t, 2)
    low, high = lax.rem(me_c, 2), me_c // 2
    near = (me_c + (1 - odd) * (1 - 2 * low) + odd * (2 - 4 * high), me_t, me_m)
    far = (me_c + odd * (1 - 2 * low) + (1 - odd) * (2 - 4 * high), me_t, me_m)
    plane = (me_c, me_t + 1 - 2 * odd, me_m)

    peers = []
    for dt in range(n_trip):
        for dc in range(n_clus):
            if dt or dc:
                peers.append((dt, dc))

    def peer_id(dt, dc):
        return (lax.rem(me_c + dc, n_clus), lax.rem(me_t + dt, n_trip), me_m)

    barrier = pltpu.get_barrier_semaphore()
    for dt, dc in peers:
        pl.semaphore_signal(barrier, inc=1, device_id=peer_id(dt, dc), device_id_type=MESH)
    pl.semaphore_signal(barrier, inc=1, device_id=sib, device_id_type=MESH)

    asked[...] = jnp.zeros_like(asked)
    for j in range(3):
        asked[j : j + 1, :] = jnp.full((1, LANES), table_ref[me_c, j].astype(f32))

    whole = half // 16 * 16
    for n in range(chunks):
        lo = n * wide
        hi = min(lo + wide, flat)
        for r in range(cl):
            at = r * rp
            if hi < lo + wide:
                edge = hi // LANES * LANES
                blocks[at : at + rp, edge : lo + wide] = jnp.zeros((rp, lo + wide - edge), bf16)
            blocks[at : at + whole, lo:hi] = force_ref[r, :whole, lo:hi]
            rest = force_ref[r, whole:, lo:hi].astype(f32)
            under = jnp.zeros((rp - half, hi - lo), f32)
            blocks[at + whole : at + rp, lo:hi] = jnp.concatenate([rest, under], axis=0).astype(bf16)

    pl.semaphore_wait(barrier, len(peers) + 1)

    def unit(k, m, n):
        return blocks.at[pl.ds(k * unit_rows, unit_rows), pl.ds(n * wide, wide)]

    started = []

    def copy_of(src, k, m, n, device):
        return pltpu.make_async_remote_copy(
            src_ref=src,
            dst_ref=zin.at[:, pl.ds(n * wide, wide)] if m else unit(k, m, n),
            send_sem=f_send.at[k, m, n],
            recv_sem=f_recv.at[k, m, n],
            device_id=device,
            device_id_type=MESH,
        )

    def send(src, k, m, n, device):
        copy = copy_of(src, k, m, n, device)
        copy.start()
        started.append(copy)

    def got(k, m, n):
        src = zout.at[:, pl.ds(n * wide, wide)] if m else unit(k, m, n)
        copy_of(src, k, m, n, sib).wait_recv()

    asks = []
    for dt in range(1, n_trip):
        copy = pltpu.make_async_remote_copy(
            src_ref=asked,
            dst_ref=wanted.at[dt],
            send_sem=t_send.at[dt],
            recv_sem=t_recv.at[dt],
            device_id=(me_c, lax.rem(me_t + dt, n_trip), me_m),
            device_id_type=MESH,
        )
        copy.start()
        asks.append(copy)
    phase_copies = []
    for k, device in ((1, near), (2, far), (3, (3 - me_c, me_t, me_m))):
        copy = pltpu.make_async_remote_copy(
            src_ref=tail_ref,
            dst_ref=tails.at[k],
            send_sem=c_send.at[k],
            recv_sem=c_recv.at[k],
            device_id=device,
            device_id_type=MESH,
        )
        copy.start()
        phase_copies.append(copy)
    for n in range(chunks):
        send(unit(0, 0, n), 1, 0, n, near)

    def answer(dt, wishes):
        target = lax.rem(me_t - dt + n_trip, n_trip)
        for j in range(3):
            wish = wishes[j : j + 1, :]
            block = jnp.zeros((ep, LANES), f32)
            for k in range(slot):
                row = send_rows_ref[0, target * slot + k]
                name = (me_t * slot + k).astype(f32)
                block = jnp.where(wish == name, eig_ref[row].astype(f32), block)
            outgoing[dt, j] = block.astype(bf16)

    answer(0, asked[...])
    eig_copies = []
    for dt in range(1, n_trip):
        asks[dt - 1].wait()
        answer(dt, wanted[dt])
    for dt in range(1, n_trip):
        copy = pltpu.make_async_remote_copy(
            src_ref=outgoing.at[dt],
            dst_ref=arrived.at[dt],
            send_sem=e_send.at[dt],
            recv_sem=e_recv.at[dt],
            device_id=(me_c, lax.rem(me_t - dt + n_trip, n_trip), me_m),
            device_id_type=MESH,
        )
        copy.start()
        eig_copies.append(copy)
    arrived[0] = outgoing[0]

    def direct(n):
        got(1, 0, n)
        send(unit(1, 0, n), 2, 0, n, plane)
        send(unit(1, 0, n), 3, 0, n, far)

    def second(n):
        got(2, 0, n)
        got(3, 0, n)

    for n in range(4):
        direct(n)
    for copy in eig_copies:
        copy.wait()
    for j in range(3):
        source = table_ref[me_c, j] // slot
        mine[j] = arrived[lax.rem(source - me_t + n_trip, n_trip), j]
    pair = pltpu.make_async_remote_copy(
        src_ref=mine,
        dst_ref=other,
        send_sem=p_send,
        recv_sem=p_recv,
        device_id=sib,
        device_id_type=MESH,
    )
    pair.start()

    pair.wait()

    first = me_m == 0

    def complex_of(j):
        a = mine[j].astype(f32)
        b = other[j].astype(f32)
        return jnp.where(first, a, b), jnp.where(first, b, a)

    re0, im0 = complex_of(0)
    re1, im1 = complex_of(1)
    re2, im2 = complex_of(2)
    f0 = re0[modes : modes + 1]
    f1, d1 = re1[modes : modes + 1], im1[modes : modes + 1]
    f2, d2 = re2[modes : modes + 1], im2[modes : modes + 1]

    def half_rows(mat, which):
        return pick(which, [mat[m * half : m * half + rp] for m in range(n_mode)])

    fill = jnp.zeros((rp - half, LANES), f32)

    def lead(mat):
        part = pick(me_m, [mat[m * half : (m + 1) * half] for m in range(n_mode)])
        turned = jnp.transpose(jnp.concatenate([part, fill] * cl, axis=0))
        return half_rows(turned, me_m), half_rows(turned, 1 - me_m)

    lead_re = lead(re0)
    lead_im = lead(im0)
    lane_k = lax.broadcasted_iota(jnp.int32, (rp, cl * rp), 1)
    lane = lax.broadcasted_iota(jnp.int32, (1, LANES), 1)

    def weights(k):
        cosines, sines = [], []
        for r in range(cl):
            tail = tail_ref[r] if k == 0 else tails[k, r]
            cosines.append(jnp.sum(jnp.where(lane == me_c, tail[0:1], 0.0), axis=1, keepdims=True))
            sines.append(jnp.sum(jnp.where(lane == me_c, tail[1:2], 0.0), axis=1, keepdims=True))
        cosv, sinv = cosines[0], sines[0]
        for r in range(1, cl):
            cosv = jnp.where(lane_k >= r * rp, cosines[r], cosv)
            sinv = jnp.where(lane_k >= r * rp, sines[r], sinv)
        at = k * unit_rows
        for h in range(2):
            wre, wim = lead_re[h], lead_im[h]
            wbuf[h * 2 * rp : (h + 1) * 2 * rp, at : at + unit_rows] = jnp.concatenate(
                [cosv * wre - sinv * wim, cosv * wim + sinv * wre], axis=0
            ).astype(bf16)

    e2a = jnp.concatenate([re2, im2], axis=1)[:modes].astype(bf16)
    e2b = jnp.concatenate([-im2, re2], axis=1)[:modes].astype(bf16)
    row_id = lax.broadcasted_iota(jnp.int32, (ep, LANES), 0)
    e1re_t = jnp.transpose(jnp.where(row_id < modes, re1, 0.0))[:ep]
    e1im_t = jnp.transpose(jnp.where(row_id < modes, im1, 0.0))[:ep]
    left[:, :ep] = jnp.concatenate([e1re_t, e1im_t], axis=0).astype(bf16)
    left[:, ep:] = jnp.concatenate([-e1im_t, e1re_t], axis=0).astype(bf16)

    def column(row):
        return jnp.transpose(jnp.broadcast_to(row, (LANES, LANES)))

    w0buf[...] = half_rows(column(f0), me_m)
    w1 = jnp.where(row_id < modes, column(f1)[:ep], 1.0)
    w2 = jnp.where(lane < modes, f2, 1.0)
    occ = jnp.where(row_id < modes, column(d1)[:ep], 0.0) + jnp.where(lane < modes, d2, 0.0)
    inverse = 1.0 / (w1 * w2)
    tre[modes * rp :, :] = jnp.zeros(((ep - modes) * rp, LANES), f32)
    tim[modes * rp :, :] = jnp.zeros(((ep - modes) * rp, LANES), f32)

    def share(n):
        cols = slice(n * wide, (n + 1) * wide)
        part = jnp.dot(wbuf[...], blocks[:, cols], preferred_element_type=f32)
        zbuf[:, cols] = part[: 2 * rp]
        zout[:, cols] = part[2 * rp :].astype(bf16)
        send(zout.at[:, pl.ds(n * wide, wide)], 0, 1, n, sib)

    def contract(n):
        got(0, 1, n)
        cols = slice(n * wide, (n + 1) * wide)
        zbuf[:, cols] = zbuf[:, cols] + zin[:, cols].astype(f32)
        for b in range(modes):
            if not n * wide < (b + 1) * modes <= (n + 1) * wide:
                continue
            part = zbuf[:, b * modes : (b + 1) * modes].astype(bf16)
            out = jnp.dot(part[:rp], e2a, preferred_element_type=f32) + jnp.dot(
                part[rp:], e2b, preferred_element_type=f32
            )
            tre[b * rp : (b + 1) * rp, :] = out[:, :LANES]
            tim[b * rp : (b + 1) * rp, :] = out[:, LANES:]

    for copy in phase_copies:
        copy.wait()
    for k in range(4):
        weights(k)

    for n in range(2, chunks + 4):
        if 4 <= n < chunks:
            direct(n)
        if 0 <= n - 2 < chunks:
            second(n - 2)
        if 0 <= n - 3 < chunks:
            share(n - 3)
        if 0 <= n - 4 < chunks:
            contract(n - 4)

    scaled = 0.5 / (smearing * smearing)
    lower = w1 + w2
    upper = w1 - w2

    def one_pair(s0):
        def rows(ref):
            return jnp.concatenate(
                [ref[pl.ds(s0 + i, ep, stride=rp), :] for i in range(2)], axis=1
            ).astype(bf16)

        both = jnp.concatenate([rows(tre), rows(tim)], axis=0)
        amp = jnp.dot(left[...], both, preferred_element_type=f32)
        square = amp * amp
        square = square[:ep] + square[ep:]
        for i in range(2):
            w0 = w0buf[pl.ds(s0 + i, 1), :]
            decays = w0 - lower
            merges = w0 + upper
            gauss = jnp.exp(-scaled * (decays * decays)) + jnp.exp(-scaled * (merges * merges))
            value = square[:, i * LANES : (i + 1) * LANES] * gauss * inverse
            at = pl.ds(pl.multiple_of((s0 + i) * 8, 8), 8)
            ratebuf[at, :] = jnp.sum(value.reshape(ep // 8, 8, LANES), axis=0)
            coupbuf[at, :] = jnp.sum((value * occ).reshape(ep // 8, 8, LANES), axis=0)

    group = 4

    def modes_step(p, carry):
        for i in range(group):
            one_pair((p * group + i) * 2)
        return carry

    lax.fori_loop(0, rp // (2 * group), modes_step, 0)

    def folded(ref):
        total = ref[pl.ds(0, rp, stride=8), :]
        for i in range(1, 8):
            total = total + ref[pl.ds(i, rp, stride=8), :]
        return jnp.sum(jnp.transpose(total), axis=0, keepdims=True)[:, :half]

    factor = mult_ref[me_c].astype(f32)
    w0_row = pick(me_m, [f0[:, m * half : (m + 1) * half] for m in range(n_mode)])
    rate = folded(ratebuf) / w0_row * factor
    coup = folded(coupbuf) / w0_row * factor
    msg[...] = jnp.zeros_like(msg)
    msg[0:1, 0:half] = rate
    msg[1:2, 0:half] = coup
    msg[2:3, :] = jnp.full((1, LANES), irr_ref[me_c].astype(f32))

    copies = []
    for index, (dt, dc) in enumerate(peers):
        copy = pltpu.make_async_remote_copy(
            src_ref=msg,
            dst_ref=inbox.at[index],
            send_sem=m_send.at[index],
            recv_sem=m_recv.at[index],
            device_id=peer_id(dt, dc),
            device_id_type=MESH,
        )
        copy.start()
        copies.append(copy)
    for copy in started:
        copy.wait_send()
    for copy in copies:
        copy.wait()

    nq = gamma_ref.shape[0]
    for q in range(nq):
        name = (me_t * nq + q).astype(f32)

        def kept(tile):
            return jnp.where(tile[2:3, :half] == name, tile[0:2, :half], 0.0)

        total = kept(msg[...])
        if len(peers) <= 16:
            for index in range(len(peers)):
                total = total + kept(inbox[index])
        else:
            total = lax.fori_loop(0, len(peers), lambda i, acc: acc + kept(inbox[i]), total)
        gamma = total[0:1] + bound_ref[q : q + 1, :]
        gamma_ref[q : q + 1, :] = gamma
        dev_ref[q : q + 1, :] = (drive_ref[q : q + 1, :] + total[1:2]) / gamma


def body(
    force_third,
    phase_angle,
    eigenvectors,
    frequencies,
    deviation,
    send_rows,
    trip_table,
    irreducible,
    multiplicity,
    drive_term,
    boundary,
):
    n_clus, n_trip, n_mode = (lax.axis_size(name) for name in ("clus", "trip", "mode"))
    cl, half, flat = force_third.shape
    points, modes, _ = eigenvectors.shape
    slot = send_rows.shape[1] // n_trip
    wide = 512
    rp = up(half, 16)
    ep = up(modes + 1, 16)
    npad = up(flat, wide)
    chunks = npad // wide
    angles = phase_angle.astype(f32)
    trig = jnp.stack([jnp.cos(angles), jnp.sin(angles)], axis=1).astype(bf16).astype(f32)
    tail = jnp.pad(trig, ((0, 0), (0, 6), (0, LANES - trig.shape[2])))
    first = lax.axis_index("mode") == 0
    part = jnp.where(first, eigenvectors[..., :modes], eigenvectors[..., modes:])
    extra = jnp.where(first, frequencies, deviation)[:, None]
    eig = jnp.pad(
        jnp.concatenate([part, extra], axis=1),
        ((0, 0), (0, ep - modes - 1), (0, LANES - modes)),
    )
    n_peers = n_clus * n_trip - 1
    vmem = pl.BlockSpec(memory_space=pltpu.VMEM)
    smem = pl.BlockSpec(memory_space=pltpu.SMEM)
    out = jax.ShapeDtypeStruct(boundary.shape, f32)
    dma = pltpu.SemaphoreType.DMA
    return tuple(
        pl.pallas_call(
            functools.partial(
                kernel, (n_clus, n_trip, n_mode, modes, half, rp, cl, slot, wide)
            ),
            out_shape=(out, out),
            in_specs=[vmem, vmem, vmem, smem, smem, smem, smem, vmem, vmem],
            out_specs=(vmem, vmem),
            scratch_shapes=[
                pltpu.VMEM((n_clus * cl * rp, npad), bf16),
                pltpu.VMEM((n_clus, cl, 8, LANES), f32),
                pltpu.VMEM((2 * n_mode * rp, n_clus * cl * rp), bf16),
                pltpu.VMEM((2 * ep, 2 * ep), bf16),
                pltpu.VMEM((8, LANES), f32),
                pltpu.VMEM((n_trip, 8, LANES), f32),
                pltpu.VMEM((n_trip, 3, ep, LANES), bf16),
                pltpu.VMEM((n_trip, 3, ep, LANES), bf16),
                pltpu.VMEM((3, ep, LANES), bf16),
                pltpu.VMEM((3, ep, LANES), bf16),
                pltpu.VMEM((2 * rp, npad), f32),
                pltpu.VMEM((2 * rp, npad), bf16),
                pltpu.VMEM((2 * rp, npad), bf16),
                pltpu.VMEM((ep * rp, LANES), f32),
                pltpu.VMEM((ep * rp, LANES), f32),
                pltpu.VMEM((rp, LANES), f32),
                pltpu.VMEM((rp * 8, LANES), f32),
                pltpu.VMEM((rp * 8, LANES), f32),
                pltpu.VMEM((8, LANES), f32),
                pltpu.VMEM((n_peers, 8, LANES), f32),
                dma((n_clus, n_mode, chunks)),
                dma((n_clus, n_mode, chunks)),
                dma((n_trip,)),
                dma((n_trip,)),
                dma((n_clus,)),
                dma((n_clus,)),
                dma((n_trip,)),
                dma((n_trip,)),
                dma,
                dma,
                dma((n_peers,)),
                dma((n_peers,)),
            ],
            compiler_params=pltpu.CompilerParams(
                collective_id=0, has_side_effects=True, vmem_limit_bytes=48 * 1024 * 1024
            ),
        )(force_third, tail, eig, send_rows, trip_table, irreducible, multiplicity, drive_term, boundary)
    )


def solution(mesh):
    return jax.shard_map(
        body,
        mesh=mesh,
        in_specs=(
            P("clus", "mode", None),
            P("clus", "trip"),
            P("trip", None, None),
            P("trip", None),
            P("trip", None),
            P("trip", None),
            P("trip", None),
            P("trip"),
            P("trip"),
            P("trip", "mode"),
            P("trip", "mode"),
        ),
        out_specs=(P("trip", "mode"), P("trip", "mode")),
        check_vma=False,
    )
```

profile of v0, /device:TPU:0, one launch (start us, length us, event | category | flops | bytes accessed | tf_op | source)
XLA Modules:
  0.0 67.7 jit_solution(13092747422451510237)
XLA Ops:
  0.6 0.0 copy-start.6
  0.6 0.8 %fusion.16 = (bf16[2,1,4]{2,0,1:T(2,128)(2,1)S(1)}, bf16[2,1,4]{2,0,1:T(2,128)(2,1)S(1)}) fusion(bf16[2,4]{1,0:T(2,128)(2,1)} %param.12), kind=kLoop, calls=%fused_computation.24 | loop fusion | flops 24 | bytes 48 | tf_op jit(solution)/shard_map/stack | solution.py:438
  1.5 0.7 %select_bitcast_fusion = bf16[8,1,90]{2,0,1:T(8,128)(2,1)S(1)} fusion(bf16[8,90]{1,0:T(8,128)(2,1)} %param.14, bf16[8,90]{1,0:T(8,128)(2,1)} %param.15, pred[]{:T(512)S(6)} %eq.3), kind=kLoop, calls=%fused_computation.18 | loop fusion | flops 720 | bytes 4321 | tf_op jit(solution)/shard_map/broadcast_in_dim | solution.py:442
  2.2 1.2 %fusion.17 = (bf16[8,90,90]{2,0,1:T(8,128)(2,1)S(1)}, bf16[8,90,90]{2,0,1:T(8,128)(2,1)S(1)}) fusion(bf16[8,90,180]{2,0,1:T(8,128)(2,1)} %param.13), kind=kLoop, calls=%fused_computation.25 | loop fusion | bytes 518400 | tf_op jit(solution)/shard_map/slice | solution.py:441
  3.4 0.1 copy_select_fusion
  3.5 0.1 fusion.5.eig_ref
  3.6 0.0 copy-done.6
  3.6 0.0 copy-start
  3.6 0.0 copy-start.1
  3.6 0.0 copy-start.2
  3.6 0.0 copy-start.3
  3.6 0.0 copy-start.4
  3.6 0.0 copy-start.5
  3.6 0.8 %copy.23.force_ref = bf16[2,45,8100]{2,1,0:T(8,128)(2,1)S(1)} copy(bf16[2,45,8100]{2,0,1:T(2,128)(2,1)S(1)} %copy-done.6) | data formatting | bytes 2916000 | tf_op args[0]
  4.5 0.0 copy-done
  4.5 0.0 copy-done.1
  4.5 0.0 copy-done.2
  4.5 0.0 copy-done.3
  4.5 0.0 copy-done.4
  4.5 0.0 copy-done.5
  4.5 62.1 %shard_map.122 = (f32[1,45]{1,0:T(1,128)S(1)}, f32[1,45]{1,0:T(1,128)S(1)}) custom-call(bf16[2,45,8100]{2,1,0:T(8,128)(2,1)S(1)} %copy.23.force_ref, f32[2,8,128]{2,1,0:T(8,128)S(1)} %fusion.12.tail_ref, bf16[8,96,128]{2,1,0:T(8,128)(2,1)S(1)} %fusion.5.eig_ref, s32[1,32]{1,0:T(1,128)S(1)} %copy-done.1, s32[4,3]{1,0:T(4,128)S(1)} %copy-done, ...), custom_call_target="tpu_custom_call" | custom-call | tf_op jit(solution)/shard_map/pallas_call | solution.py:453
  66.7 0.5 copy.30
  67.2 0.5 copy.31
  (4 shorter events, 0.0 us)
Async XLA Ops:
  0.6 2.9 %copy-start.6 = (bf16[2,45,8100]{2,0,1:T(2,128)(2,1)S(1)}, bf16[2,45,8100]{2,0,1:T(2,128)(2,1)}, u32[]{:S(2)}) copy-start(bf16[2,45,8100]{2,0,1:T(2,128)(2,1)} %param.11) | copy-start | bytes 4374004
  3.6 0.9 %copy-start = (s32[4,3]{1,0:T(4,128)S(1)}, s32[4,3]{1,0:T(4,128)}, u32[]{:S(2)}) copy-start(s32[4,3]{1,0:T(4,128)} %table_ref.1) | copy-start | bytes 148
  3.6 0.9 %copy-start.1 = (s32[1,32]{1,0:T(1,128)S(1)}, s32[1,32]{1,0:T(1,128)}, u32[]{:S(2)}) copy-start(s32[1,32]{1,0:T(1,128)} %send_rows_ref.1) | copy-start | bytes 388
  3.6 0.9 %copy-start.2 = (s32[4]{0:T(128)S(1)}, s32[4]{0:T(128)}, u32[]{:S(2)}) copy-start(s32[4]{0:T(128)} %irr_ref.1) | copy-start | bytes 52
  3.6 0.9 %copy-start.3 = (s32[4]{0:T(128)S(1)}, s32[4]{0:T(128)}, u32[]{:S(2)}) copy-start(s32[4]{0:T(128)} %mult_ref.1) | copy-start | bytes 52
  3.6 0.9 %copy-start.4 = (f32[1,45]{1,0:T(1,128)S(1)}, f32[1,45]{1,0:T(1,128)}, u32[]{:S(2)}) copy-start(f32[1,45]{1,0:T(1,128)} %drive_ref.1) | copy-start | bytes 544
  3.6 0.9 %copy-start.5 = (f32[1,45]{1,0:T(1,128)S(1)}, f32[1,45]{1,0:T(1,128)}, u32[]{:S(2)}) copy-start(f32[1,45]{1,0:T(1,128)} %bound_ref.1) | copy-start | bytes 544
where the time goes:
time: 67.9 us; the launch traced here: 67.7 us
  Pallas kernels  62.1 us (91%)
  local copies, waits for them, and re-layouts  3.11 us (5%)
  other arithmetic  1.65 us (2%)
  between operations  0.8 us (1%)
    pallas_call x1, Pallas kernels, body(): pl.pallas_call(functools.partial(kernel, (n_clus, n_trip, n_mode, modes,...  62.1 us
    unnamed x17, local copies, waits for them, and re-layouts  1.89 us

commit v1 on v0

v1 whole, which is shorter than its diff:
```python
import functools

import jax
import jax.numpy as jnp
from jax import lax
from jax.experimental import pallas as pl
from jax.experimental.pallas import tpu as pltpu
from jax.sharding import PartitionSpec as P

smearing = 0.3
MESH = pl.DeviceIdType.MESH
LANES = 128
SUB = 16
WORKERS = 8
f32 = jnp.float32
bf16 = jnp.bfloat16


def up(value, step):
    return -(-value // step) * step


def pick(index, options):
    chosen = options[0]
    for position in range(1, len(options)):
        chosen = jnp.where(index == position, options[position], chosen)
    return chosen


def flip(bit, by):
    return bit + by - 2 * bit * by


def plan(flat):
    left = -(-flat // (WORKERS * LANES))
    units = [1] if left > 2 else []
    left -= sum(units)
    while left > 0:
        units.append(min(2, left))
        left -= units[-1]
    rounds, base, col = [], 0, 0
    for index, unit in enumerate(units):
        rounds.append((index % 2, base, unit * LANES, col))
        base += unit * LANES * WORKERS
        col += unit * LANES
    return rounds


def kernel(
    dims,
    force_ref,
    angle_ref,
    eig_ref,
    freq_ref,
    occ_ref,
    send_rows_ref,
    table_ref,
    irr_ref,
    mult_ref,
    drive_ref,
    bound_ref,
    gamma_ref,
    dev_ref,
    own,
    fbuf,
    gout,
    gin,
    gsib,
    tails,
    lset,
    wphase,
    wz,
    left,
    ehalf,
    asked,
    wanted,
    outgoing,
    arrived,
    mine,
    other,
    ebuf,
    zbuf,
    tre,
    tim,
    w0buf,
    gauss,
    ratebuf,
    coupbuf,
    msg,
    inbox,
    f_send,
    f_recv,
    g_send,
    g_recv,
    s_send,
    s_recv,
    t_send,
    t_recv,
    c_send,
    c_recv,
    e_send,
    e_recv,
    p_send,
    p_recv,
    m_send,
    m_recv,
):
    n_clus, n_trip, n_mode, modes, half, rp, cl, slot, rounds = dims
    ep = up(modes + 1, 16)
    flat = force_ref.shape[2]
    wide = own.shape[1]
    c = lax.axis_index("clus")
    t = lax.axis_index("trip")
    m = lax.axis_index("mode")
    k = lax.rem(t, 2)
    tz = t + 1 - 2 * k
    bits = (lax.rem(c, 2), c // 2)
    step = (1 - 2 * bits[0], 2 - 4 * bits[1])
    sib = (c, t, 1 - m)
    first = m == 0

    peers = []
    for dt in range(n_trip):
        for dc in range(n_clus):
            if dt or dc:
                peers.append((dt, dc))

    def peer_id(dt, dc):
        return (lax.rem(c + dc, n_clus), lax.rem(t + dt, n_trip), m)

    def clus_at(axis, du):
        return c + step[axis] if du else c

    across = [sib]
    for axis in range(2):
        for dk in range(2):
            across.append((clus_at(axis, 1), tz if dk else t, 1 - m))
    across.append((c, tz, 1 - m))

    barrier = pltpu.get_barrier_semaphore()
    for dt, dc in peers:
        pl.semaphore_signal(barrier, inc=1, device_id=peer_id(dt, dc), device_id_type=MESH)
    for device in across:
        pl.semaphore_signal(barrier, inc=1, device_id=device, device_id_type=MESH)

    asked[...] = jnp.zeros_like(asked)
    for j in range(3):
        asked[j : j + 1, :] = jnp.full((1, LANES), table_ref[c, j].astype(f32))

    whole = half // 16 * 16
    edge = flat // LANES * LANES
    for r in range(cl):
        at = r * rp
        if edge < wide:
            own[at : at + rp, edge:wide] = jnp.zeros((rp, wide - edge), bf16)
        own[at : at + whole, :flat] = force_ref[r, :whole, :]
        rest = force_ref[r, whole:, :].astype(f32)
        under = jnp.zeros((rp - half, flat), f32)
        own[at + whole : at + rp, :flat] = jnp.concatenate([rest, under], axis=0).astype(bf16)

    angles = angle_ref[...].astype(f32)
    here = k * n_clus + c
    tails[here] = jnp.zeros((8, LANES), f32)
    tails[here, 0:cl, 0 : angles.shape[1]] = jnp.cos(angles).astype(bf16).astype(f32)
    tails[here, cl : 2 * cl, 0 : angles.shape[1]] = jnp.sin(angles).astype(bf16).astype(f32)

    points = eig_ref.shape[0]
    ehalf[...] = jnp.zeros_like(ehalf)
    for p in range(points):
        both = eig_ref[p].astype(f32)
        ehalf[p, 0:half, 0 : 2 * modes] = pick(m, [both[h * half : (h + 1) * half] for h in range(n_mode)])
    extra = jnp.where(first, freq_ref[...].astype(f32), occ_ref[...].astype(f32))
    for p in range(points):
        ehalf[p, half : half + 1, 0:modes] = extra[p : p + 1]

    pl.semaphore_wait(barrier, len(peers) + len(across))

    started = []

    def remote(src, dst, send_sem, recv_sem, device):
        return pltpu.make_async_remote_copy(
            src_ref=src,
            dst_ref=dst,
            send_sem=send_sem,
            recv_sem=recv_sem,
            device_id=device,
            device_id_type=MESH,
        )

    def send(src, dst, send_sem, recv_sem, device):
        copy = remote(src, dst, send_sem, recv_sem, device)
        copy.start()
        started.append(copy)

    asks = []
    for dt in range(1, n_trip):
        copy = remote(asked, wanted.at[dt], t_send.at[dt], t_recv.at[dt], (c, lax.rem(t + dt, n_trip), m))
        copy.start()
        asks.append(copy)

    cube = []
    cube_clus = [c, c + step[0], c + step[1], c + step[0] + step[1]]
    for dk in range(2):
        for dc in range(n_clus):
            if dk or dc:
                cube.append((dk, dc))
    for index, (dk, dc) in enumerate(cube):
        send(
            tails.at[here],
            tails.at[here],
            c_send.at[index],
            c_recv.at[here],
            (cube_clus[dc], tz if dk else t, m),
        )

    def worker(ub, kk, mm):
        return (ub * 2 + kk) * 2 + mm

    def columns(e, w):
        _, base, width, _ = rounds[e]
        return pl.ds(pl.multiple_of(base + w * width, LANES), width)

    def local(e):
        return pl.ds(rounds[e][3], rounds[e][2])

    def lines(e):
        axis = rounds[e][0]
        cu, cv = clus_at(axis, 1), clus_at(1 - axis, 1)
        return bits[axis], cu, cv, c + step[0] + step[1]

    def direct(e):
        ub, cu, cv, _ = lines(e)
        dst = fbuf.at[m, c, :, local(e)]
        recv = f_recv.at[e, m, c]
        for index, mm in enumerate((m, 1 - m)):
            send(own.at[:, columns(e, worker(1 - ub, k, mm))], dst, f_send.at[e, index], recv, (cu, t, mm))
            send(own.at[:, columns(e, worker(ub, k, mm))], dst, f_send.at[e, 2 + index], recv, (cv, t, mm))
        send(own.at[:, columns(e, worker(ub, k, 1 - m))], dst, f_send.at[e, 4], recv, sib)

    def got(e, g, cc):
        ref = fbuf.at[g, cc, :, local(e)]
        remote(ref, ref, f_send.at[e, 0], f_recv.at[e, g, cc], sib).wait_recv()

    def forward(e):
        _, cu, cv, _ = lines(e)
        for g in range(n_mode):
            got(e, g, cu)
            ref = fbuf.at[g, cu, :, local(e)]
            send(ref, ref, f_send.at[e, 5 + g], f_recv.at[e, g, cu], (cv, t, m))

    def phased(e):
        axis = rounds[e][0]
        ub, _, cv, cd = lines(e)
        me = worker(ub, k, m)
        fbuf[m, c, :, local(e)] = own[:, columns(e, me)]
        got(e, 1 - m, c)
        for g in range(n_mode):
            got(e, g, cv)
            got(e, g, cd)
        weights = wphase[axis]
        for g in range(n_mode):
            for a0 in range(0, rp, SUB):
                parts = []
                for cc in range(n_clus):
                    for r in range(cl):
                        parts.append(fbuf[g, cc, r * rp + a0 : r * rp + a0 + SUB, local(e)])
                out = jnp.dot(weights, jnp.concatenate(parts, axis=0), preferred_element_type=f32).astype(bf16)
                for q in range(4):
                    for i in range(2):
                        row = (q * 2 + i) * SUB
                        gout[q, g, i * rp + a0 : i * rp + a0 + SUB, local(e)] = out[row : row + SUB]
        dst = gin.at[:, columns(e, me)]
        recv = g_recv.at[e, me]
        index = 0
        for du, dk in ((1, 1), (0, 1), (1, 0)):
            for g in range(n_mode):
                device = (clus_at(axis, du), tz if dk else t, g)
                send(gout.at[du * 2 + dk, g, :, local(e)], dst, g_send.at[e, index], recv, device)
                index += 1
        send(gout.at[0, 1 - m, :, local(e)], dst, g_send.at[e, index], recv, sib)
        gin[:, columns(e, me)] = gout[0, m, :, local(e)]

    def gather(e):
        axis, base, width, _ = rounds[e]
        ub = bits[axis]
        for du in range(2):
            for dk in range(2):
                for dm in range(2):
                    if du or dk or dm:
                        w = worker(flip(ub, du), flip(k, dk), flip(m, dm))
                        ref = gin.at[:, columns(e, w)]
                        remote(ref, ref, g_send.at[e, 0], g_recv.at[e, w], sib).wait_recv()
        span = pl.ds(base, WORKERS * width)
        send(gin.at[:, span], gsib.at[:, span], s_send.at[e], s_recv.at[e], sib)

    def answer(dt, wishes):
        target = lax.rem(t - dt + n_trip, n_trip)
        for j in range(3):
            wish = wishes[j : j + 1, 0:1]
            block = jnp.zeros(ehalf.shape[1:], f32)
            for p in range(slot):
                row = send_rows_ref[0, target * slot + p]
                name = (t * slot + p).astype(f32)
                block = jnp.where(wish == name, ehalf[row], block)
            outgoing[dt, j] = block.astype(bf16)

    eig_copies = []

    def answers():
        for dt in range(1, n_trip):
            asks[dt - 1].wait()
            answer(dt, wanted[dt])
        for dt in range(1, n_trip):
            copy = remote(
                outgoing.at[dt],
                arrived.at[dt],
                e_send.at[dt],
                e_recv.at[dt],
                (c, lax.rem(t - dt + n_trip, n_trip), m),
            )
            copy.start()
            eig_copies.append(copy)
        answer(0, asked[...])
        arrived[0] = outgoing[0]

    lane = lax.broadcasted_iota(jnp.int32, (1, LANES), 1)

    def phase_weights():
        for dk, dc in cube:
            there = flip(k, dk) * n_clus + cube_clus[dc]
            ref = tails.at[there]
            remote(ref, ref, c_send.at[0], c_recv.at[there], sib).wait_recv()
        stack = jnp.concatenate([tails[i] for i in range(2 * n_clus)], axis=0)
        stack = jnp.concatenate([stack, jnp.zeros((LANES - stack.shape[0], LANES), f32)], axis=0)
        turned = jnp.transpose(stack)[:SUB].astype(bf16)
        row = lax.broadcasted_iota(jnp.int32, (LANES, LANES), 0)
        col = lax.broadcasted_iota(jnp.int32, (LANES, LANES), 1)
        source = (col // (cl * SUB)) * 8 + lax.rem(col // SUB, cl)
        for kk in range(2):
            for i in range(2):
                spread = jnp.where(row == source + (kk * n_clus * 8 + i * cl), 1.0, 0.0).astype(bf16)
                lset[kk * 2 + i] = jnp.dot(turned, spread, preferred_element_type=f32)
        same = lax.broadcasted_iota(jnp.int32, (SUB, LANES), 0) == lax.rem(
            lax.broadcasted_iota(jnp.int32, (SUB, LANES), 1), SUB
        )
        for axis in range(2):
            for du in range(2):
                for dk in range(2):
                    for i in range(2):
                        values = lset[flip(k, dk) * 2 + i, pl.ds(clus_at(axis, du), 1), :]
                        at = ((du * 2 + dk) * 2 + i) * SUB
                        wphase[axis, at : at + SUB, :] = jnp.where(same, values, 0.0).astype(bf16)

    pair = remote(mine, other, p_send, p_recv, sib)

    def members():
        for copy in eig_copies:
            copy.wait()
        for j in range(3):
            source = table_ref[c, j] // slot
            mine[j] = arrived[lax.rem(source - t + n_trip, n_trip), j]
        pair.start()

    fill = jnp.zeros((LANES - 2 * rp, LANES), f32)
    state = {}

    def half_rows(mat, which):
        return pick(which, [mat[h * half : h * half + rp] for h in range(n_mode)])

    def column(row):
        return jnp.transpose(jnp.broadcast_to(row, (LANES, LANES)))

    def vectors():
        pair.wait()
        ebuf[...] = jnp.zeros_like(ebuf)
        freqs, occs = [], []
        for j in range(3):
            a = mine[j].astype(f32)
            b = other[j].astype(f32)
            parts = jnp.where(first, a, b), jnp.where(first, b, a)
            for g in range(n_mode):
                at = g * rp if j == 0 else g * half
                ebuf[j, 0, at : at + half, 0:modes] = parts[g][:half, 0:modes]
                ebuf[j, 1, at : at + half, 0:modes] = parts[g][:half, modes : 2 * modes]
            w0buf[2 * j : 2 * j + 1, 0:LANES] = parts[0][half : half + 1, 0:LANES]
            w0buf[2 * j + 1 : 2 * j + 2, 0:LANES] = parts[1][half : half + 1, 0:LANES]
            freqs.append(w0buf[2 * j : 2 * j + 1, :])
            occs.append(w0buf[2 * j + 1 : 2 * j + 2, :])
        f0, f1, f2 = freqs
        _, d1, d2 = occs
        for place, g in enumerate((m, 1 - m)):
            re0 = ebuf[0, 0, pl.ds(pl.multiple_of(g * rp, 16), rp), :]
            im0 = ebuf[0, 1, pl.ds(pl.multiple_of(g * rp, 16), rp), :]
            real = half_rows(jnp.transpose(jnp.concatenate([re0, -im0, fill], axis=0)), m)
            imag = half_rows(jnp.transpose(jnp.concatenate([im0, re0, fill], axis=0)), m)
            turned = jnp.concatenate([real, imag], axis=0)[:, : 2 * rp].astype(bf16)
            wz[:, place * 2 * rp : (place + 1) * 2 * rp] = turned
        re1, im1 = ebuf[1, 0], ebuf[1, 1]
        re2, im2 = ebuf[2, 0], ebuf[2, 1]
        state["e2a"] = jnp.concatenate([re2, im2], axis=1)[:modes].astype(bf16)
        state["e2b"] = jnp.concatenate([-im2, re2], axis=1)[:modes].astype(bf16)
        tall = jnp.zeros((LANES - ep, LANES), f32)
        e1re_t = jnp.transpose(jnp.concatenate([re1, tall], axis=0))[:ep, :ep]
        e1im_t = jnp.transpose(jnp.concatenate([im1, tall], axis=0))[:ep, :ep]
        left[:, :ep] = jnp.concatenate([e1re_t, e1im_t], axis=0).astype(bf16)
        left[:, ep:] = jnp.concatenate([-e1im_t, e1re_t], axis=0).astype(bf16)
        row_id = lax.broadcasted_iota(jnp.int32, (ep, LANES), 0)
        state["w0row"] = f0
        state["w0"] = half_rows(column(f0), m)
        w1 = jnp.where(row_id < modes, column(f1)[:ep], 1.0)
        w2 = jnp.where(lane < modes, f2, 1.0)
        state["occ"] = jnp.where(row_id < modes, column(d1)[:ep], 0.0) + jnp.where(lane < modes, d2, 0.0)
        state["inverse"] = 1.0 / (w1 * w2)
        state["lower"] = w1 + w2
        state["upper"] = w1 - w2
        tre[modes * rp :, :] = jnp.zeros(((ep - modes) * rp, LANES), f32)
        tim[modes * rp :, :] = jnp.zeros(((ep - modes) * rp, LANES), f32)
        w0buf[8:, :] = state["w0"]

    scaled = 0.5 / (smearing * smearing)

    def gaussians(lo, hi):
        lower, upper, inverse = state["lower"], state["upper"], state["inverse"]

        def one(s, carry):
            w0 = w0buf[pl.ds(8 + s, 1), :]
            decays = w0 - lower
            merges = w0 + upper
            both = jnp.exp(-scaled * (decays * decays)) + jnp.exp(-scaled * (merges * merges))
            gauss[s] = both * inverse
            return carry

        lax.fori_loop(lo, hi, one, 0)

    def contract(e):
        _, base, width, _ = rounds[e]
        lo, hi = base, base + WORKERS * width
        span = pl.ds(lo, hi - lo)
        ref = gsib.at[:, span]
        remote(ref, ref, s_send.at[e], s_recv.at[e], sib).wait_recv()
        for at in range(lo, hi, 512):
            cols = slice(at, at + 512)
            both = jnp.concatenate([gin[:, cols], gsib[:, cols]], axis=0)
            zbuf[:, cols] = jnp.dot(wz[...], both, preferred_element_type=f32)
        for b in range(modes):
            if not lo < (b + 1) * modes <= hi:
                continue
            part = zbuf[:, b * modes : (b + 1) * modes].astype(bf16)
            out = jnp.dot(part[:rp], state["e2a"], preferred_element_type=f32) + jnp.dot(
                part[rp:], state["e2b"], preferred_element_type=f32
            )
            tre[b * rp : (b + 1) * rp, :] = out[:, :LANES]
            tim[b * rp : (b + 1) * rp, :] = out[:, LANES:]

    total = len(rounds)

    direct(0)
    if total > 1:
        direct(1)
    forward(0)
    if total > 2:
        direct(2)
    answers()
    phase_weights()
    for e in range(total):
        if e + 1 < total:
            forward(e + 1)
        if e + 3 < total:
            direct(e + 3)
        phased(e)
        if e == 1:
            members()
        if e == 2:
            gather(0)
            vectors()
        if e >= 3:
            gather(e - 2)
            contract(e - 3)
            gaussians((e - 3) * rp // 2, (e - 2) * rp // 2)
    gaussians(max(total - 3, 0) * rp // 2, rp)
    for e in range(max(total - 3, 0), total):
        if e + 1 < total:
            gather(e + 1)
        contract(e)

    occ = state["occ"]

    def one_pair(s0):
        def rows(ref):
            return jnp.concatenate(
                [ref[pl.ds(s0 + i, ep, stride=rp), :] for i in range(2)], axis=1
            ).astype(bf16)

        both = jnp.concatenate([rows(tre), rows(tim)], axis=0)
        amp = jnp.dot(left[...], both, preferred_element_type=f32)
        square = amp * amp
        square = square[:ep] + square[ep:]
        for i in range(2):
            value = square[:, i * LANES : (i + 1) * LANES] * gauss[s0 + i]
            at = pl.ds(pl.multiple_of((s0 + i) * 8, 8), 8)
            ratebuf[at, :] = jnp.sum(value.reshape(ep // 8, 8, LANES), axis=0)
            coupbuf[at, :] = jnp.sum((value * occ).reshape(ep // 8, 8, LANES), axis=0)

    group = 4

    def modes_step(p, carry):
        for i in range(group):
            one_pair((p * group + i) * 2)
        return carry

    lax.fori_loop(0, rp // (2 * group), modes_step, 0)

    def folded(ref):
        total = ref[pl.ds(0, rp, stride=8), :]
        for i in range(1, 8):
            total = total + ref[pl.ds(i, rp, stride=8), :]
        return jnp.sum(jnp.transpose(total), axis=0, keepdims=True)[:, :half]

    factor = mult_ref[c].astype(f32)
    f0 = state["w0row"]
    w0_row = pick(m, [f0[:, h * half : (h + 1) * half] for h in range(n_mode)])
    rate = folded(ratebuf) / w0_row * factor
    coup = folded(coupbuf) / w0_row * factor
    msg[...] = jnp.zeros_like(msg)
    msg[0:1, 0:half] = rate
    msg[1:2, 0:half] = coup
    msg[2:3, :] = jnp.full((1, LANES), irr_ref[c].astype(f32))

    copies = []
    for index, (dt, dc) in enumerate(peers):
        copy = remote(msg, inbox.at[index], m_send.at[index], m_recv.at[index], peer_id(dt, dc))
        copy.start()
        copies.append(copy)
    for copy in started:
        copy.wait_send()
    for copy in copies:
        copy.wait()

    nq = gamma_ref.shape[0]
    for q in range(nq):
        name = (t * nq + q).astype(f32)

        def kept(tile):
            return jnp.where(tile[2:3, :half] == name, tile[0:2, :half], 0.0)

        total = kept(msg[...])
        if len(peers) <= 16:
            for index in range(len(peers)):
                total = total + kept(inbox[index])
        else:
            total = lax.fori_loop(0, len(peers), lambda i, acc: acc + kept(inbox[i]), total)
        gamma = total[0:1] + bound_ref[q : q + 1, :]
        gamma_ref[q : q + 1, :] = gamma
        dev_ref[q : q + 1, :] = (drive_ref[q : q + 1, :] + total[1:2]) / gamma


def body(
    force_third,
    phase_angle,
    eigenvectors,
    frequencies,
    deviation,
    send_rows,
    trip_table,
    irreducible,
    multiplicity,
    drive_term,
    boundary,
):
    n_clus, n_trip, n_mode = (lax.axis_size(name) for name in ("clus", "trip", "mode"))
    cl, half, flat = force_third.shape
    points, modes, _ = eigenvectors.shape
    slot = send_rows.shape[1] // n_trip
    rounds = plan(flat)
    count = len(rounds)
    rp = up(half, 16)
    ep = up(modes + 1, 16)
    share = sum(width for _, _, width, _ in rounds)
    npad = share * WORKERS
    elanes = up(2 * modes, LANES)
    n_peers = n_clus * n_trip - 1
    vmem = pl.BlockSpec(memory_space=pltpu.VMEM)
    smem = pl.BlockSpec(memory_space=pltpu.SMEM)
    out = jax.ShapeDtypeStruct(boundary.shape, f32)
    dma = pltpu.SemaphoreType.DMA
    return tuple(
        pl.pallas_call(
            functools.partial(kernel, (n_clus, n_trip, n_mode, modes, half, rp, cl, slot, rounds)),
            out_shape=(out, out),
            in_specs=[vmem, vmem, vmem, vmem, vmem, smem, smem, smem, smem, vmem, vmem],
            out_specs=(vmem, vmem),
            scratch_shapes=[
                pltpu.VMEM((cl * rp, npad), bf16),
                pltpu.VMEM((n_mode, n_clus, cl * rp, share), bf16),
                pltpu.VMEM((4, n_mode, 2 * rp, share), bf16),
                pltpu.VMEM((2 * rp, npad), bf16),
                pltpu.VMEM((2 * rp, npad), bf16),
                pltpu.VMEM((2 * n_clus, 8, LANES), f32),
                pltpu.VMEM((4, SUB, LANES), f32),
                pltpu.VMEM((2, LANES, LANES), bf16),
                pltpu.VMEM((2 * rp, 2 * n_mode * rp), bf16),
                pltpu.VMEM((2 * ep, 2 * ep), bf16),
                pltpu.VMEM((points, rp, elanes), f32),
                pltpu.VMEM((8, LANES), f32),
                pltpu.VMEM((n_trip, 8, LANES), f32),
                pltpu.VMEM((n_trip, 3, rp, elanes), bf16),
                pltpu.VMEM((n_trip, 3, rp, elanes), bf16),
                pltpu.VMEM((3, rp, elanes), bf16),
                pltpu.VMEM((3, rp, elanes), bf16),
                pltpu.VMEM((3, 2, ep, LANES), f32),
                pltpu.VMEM((2 * rp, npad), f32),
                pltpu.VMEM((ep * rp, LANES), f32),
                pltpu.VMEM((ep * rp, LANES), f32),
                pltpu.VMEM((8 + rp, LANES), f32),
                pltpu.VMEM((rp, ep, LANES), f32),
                pltpu.VMEM((rp * 8, LANES), f32),
                pltpu.VMEM((rp * 8, LANES), f32),
                pltpu.VMEM((8, LANES), f32),
                pltpu.VMEM((n_peers, 8, LANES), f32),
                dma((count, 7)),
                dma((count, n_mode, n_clus)),
                dma((count, 7)),
                dma((count, WORKERS)),
                dma((count,)),
                dma((count,)),
                dma((n_trip,)),
                dma((n_trip,)),
                dma((2 * n_clus,)),
                dma((2 * n_clus,)),
                dma((n_trip,)),
                dma((n_trip,)),
                dma,
                dma,
                dma((n_peers,)),
                dma((n_peers,)),
            ],
            compiler_params=pltpu.CompilerParams(
                collective_id=0, has_side_effects=True, vmem_limit_bytes=48 * 1024 * 1024
            ),
        )(
            force_third,
            phase_angle,
            eigenvectors,
            frequencies,
            deviation,
            send_rows,
            trip_table,
            irreducible,
            multiplicity,
            drive_term,
            boundary,
        )
    )


def solution(mesh):
    return jax.shard_map(
        body,
        mesh=mesh,
        in_specs=(
            P("clus", "mode", None),
            P("clus", "trip"),
            P("trip", None, None),
            P("trip", None),
            P("trip", None),
            P("trip", None),
            P("trip", None),
            P("trip"),
            P("trip"),
            P("trip", "mode"),
            P("trip", "mode"),
        ),
        out_specs=(P("trip", "mode"), P("trip", "mode")),
        check_vma=False,
    )
```

time: 67.9 us -> 50.3 us (0.74)
  Pallas kernels: 62.1 us -> 45 us
  other arithmetic: 1.65 us -> 0 us
  local copies, waits for them, and re-layouts: 3.11 us -> 4.37 us
    pallas_call x1, Pallas kernels: 62.1 us -> 45 us  [body(): pl.pallas_call(functools.partial(kernel, (n_clus, n_trip, n_mode, modes,...]
    unnamed x17 -> x22, local copies, waits for them, and re-layouts: 1.89 us -> 4.37 us
    slice x1 -> x0, local copies, waits for them, and re-layouts: 1.21 us -> none  [body(): eigenvectors[..., :modes]]
    another operation x1 -> x0, other arithmetic: 0.81 us -> none  [body(): jnp.stack([jnp.cos(angles), jnp.sin(angles)], axis=1).astype(bf16)]
    broadcast_in_dim x1 -> x0, other arithmetic: 0.7 us -> none  [body(): extra = jnp.where(first, frequencies, deviation)[:, None]]
where the time goes in v1:
time: 50.3 us; the launch traced here: 50.1 us
  Pallas kernels  45 us (89%)
  local copies, waits for them, and re-layouts  4.37 us (9%)
  between operations  0.79 us (2%)
    pallas_call x1, Pallas kernels, body(): pl.pallas_call(functools.partial(kernel, (n_clus, n_trip, n_mode, modes,...  45 us
    unnamed x22, local copies, waits for them, and re-layouts  4.37 us

profile of v1, /device:TPU:0, one launch (start us, length us, event | category | flops | bytes accessed | tf_op | source)
XLA Modules:
  0.0 50.1 jit_solution(5789793035903754638)
XLA Ops:
  0.6 1.1 %copy.14.eig_ref = bf16[8,90,180]{2,1,0:T(8,128)(2,1)S(1)} copy(bf16[8,90,180]{2,0,1:T(8,128)(2,1)} %param.13) | data formatting | bytes 518400 | tf_op args[2]
  1.7 0.0 copy-start
  1.7 0.0 copy-start.1
  1.7 0.0 copy-start.2
  1.7 0.0 copy-start.3
  1.7 0.0 copy-start.4
  1.8 0.0 copy-start.5
  1.8 0.0 copy-start.6
  1.8 0.0 copy-start.7
  1.8 0.0 copy-start.8
  1.8 2.2 %copy.13.force_ref = bf16[2,45,8100]{2,1,0:T(8,128)(2,1)S(1)} copy(bf16[2,45,8100]{2,0,1:T(2,128)(2,1)} %param.11) | data formatting | bytes 2916000 | tf_op args[0]
  4.0 0.0 copy-done
  4.0 0.0 copy-done.1
  4.1 0.0 copy-done.2
  4.1 0.0 copy-done.3
  4.1 0.0 copy-done.4
  4.1 0.0 copy-done.5
  4.1 0.0 copy-done.6
  4.1 0.0 copy-done.7
  4.1 0.0 copy-done.8
  4.1 45.0 %shard_map.122 = (f32[1,45]{1,0:T(1,128)S(1)}, f32[1,45]{1,0:T(1,128)S(1)}) custom-call(bf16[2,45,8100]{2,1,0:T(8,128)(2,1)S(1)} %copy.13.force_ref, bf16[2,4]{1,0:T(2,128)(2,1)S(1)} %copy-done.3, bf16[8,90,180]{2,1,0:T(8,128)(2,1)S(1)} %copy.14.eig_ref, bf16[8,90]{1,0:T(8,128)(2,1)S(1)} %copy-done, bf16[8,90]{1,0:T(8,128)(2,1)S(1)} %copy-done.1, ...), custom_call_target="tpu_custom_call" | custom-call | tf_op jit(solution)/shard_map/pallas_call | solution.py:587
  49.1 0.5 %copy.17 = f32[1,45]{1,0:T(1,128)} copy(f32[1,45]{1,0:T(1,128)S(1)} %get-tuple-element.4) | data formatting | bytes 360
  49.6 0.5 %copy.18 = f32[1,45]{1,0:T(1,128)} copy(f32[1,45]{1,0:T(1,128)S(1)} %get-tuple-element.5) | data formatting | bytes 360
Async XLA Ops:
  1.7 2.3 %copy-start = (bf16[8,90]{1,0:T(8,128)(2,1)S(1)}, bf16[8,90]{1,0:T(8,128)(2,1)}, u32[]{:S(2)}) copy-start(bf16[8,90]{1,0:T(8,128)(2,1)} %freq_ref.1) | copy-start | bytes 4324
  1.7 2.3 %copy-start.1 = (bf16[8,90]{1,0:T(8,128)(2,1)S(1)}, bf16[8,90]{1,0:T(8,128)(2,1)}, u32[]{:S(2)}) copy-start(bf16[8,90]{1,0:T(8,128)(2,1)} %occ_ref.1) | copy-start | bytes 4324
  1.7 2.3 %copy-start.2 = (s32[4,3]{1,0:T(4,128)S(1)}, s32[4,3]{1,0:T(4,128)}, u32[]{:S(2)}) copy-start(s32[4,3]{1,0:T(4,128)} %table_ref.1) | copy-start | bytes 148
  1.7 2.3 %copy-start.3 = (bf16[2,4]{1,0:T(2,128)(2,1)S(1)}, bf16[2,4]{1,0:T(2,128)(2,1)}, u32[]{:S(2)}) copy-start(bf16[2,4]{1,0:T(2,128)(2,1)} %angle_ref.1) | copy-start | bytes 52
  1.7 2.3 %copy-start.4 = (s32[1,32]{1,0:T(1,128)S(1)}, s32[1,32]{1,0:T(1,128)}, u32[]{:S(2)}) copy-start(s32[1,32]{1,0:T(1,128)} %send_rows_ref.1) | copy-start | bytes 388
  1.8 2.3 %copy-start.5 = (s32[4]{0:T(128)S(1)}, s32[4]{0:T(128)}, u32[]{:S(2)}) copy-start(s32[4]{0:T(128)} %irr_ref.1) | copy-start | bytes 52
  1.8 2.3 %copy-start.6 = (s32[4]{0:T(128)S(1)}, s32[4]{0:T(128)}, u32[]{:S(2)}) copy-start(s32[4]{0:T(128)} %mult_ref.1) | copy-start | bytes 52
  1.8 2.3 %copy-start.7 = (f32[1,45]{1,0:T(1,128)S(1)}, f32[1,45]{1,0:T(1,128)}, u32[]{:S(2)}) copy-start(f32[1,45]{1,0:T(1,128)} %drive_ref.1) | copy-start | bytes 544
  1.8 2.3 %copy-start.8 = (f32[1,45]{1,0:T(1,128)S(1)}, f32[1,45]{1,0:T(1,128)}, u32[]{:S(2)}) copy-start(f32[1,45]{1,0:T(1,128)} %bound_ref.1) | copy-start | bytes 544

commit v2 on v1

--- a/solution.py
+++ b/solution.py
@@ -12,6 +12,8 @@
 LANES = 128
 SUB = 16
 WORKERS = 8
+NEAR = 0
+VMEM_BYTES = 66 * 1000 * 1000
 f32 = jnp.float32
 bf16 = jnp.bfloat16
 
@@ -40,7 +42,7 @@
         left -= units[-1]
     rounds, base, col = [], 0, 0
     for index, unit in enumerate(units):
-        rounds.append((index % 2, base, unit * LANES, col))
+        rounds.append((index % 2, base, unit * LANES, col, index < NEAR))
         base += unit * LANES * WORKERS
         col += unit * LANES
     return rounds
@@ -49,8 +51,18 @@
 def kernel(
     dims,
     force_ref,
+    eig_ref,
+    angle_hbm,
+    freq_hbm,
+    occ_hbm,
+    send_rows_hbm,
+    table_hbm,
+    irr_hbm,
+    mult_hbm,
+    drive_hbm,
+    bound_hbm,
+    out_ref,
     angle_ref,
-    eig_ref,
     freq_ref,
     occ_ref,
     send_rows_ref,
@@ -59,8 +71,8 @@
     mult_ref,
     drive_ref,
     bound_ref,
-    gamma_ref,
-    dev_ref,
+    lin,
+    elin,
     own,
     fbuf,
     gout,
@@ -104,10 +116,11 @@
     p_recv,
     m_send,
     m_recv,
+    l_sem,
 ):
     n_clus, n_trip, n_mode, modes, half, rp, cl, slot, rounds = dims
     ep = up(modes + 1, 16)
-    flat = force_ref.shape[2]
+    flat = lin.shape[2]
     wide = own.shape[1]
     c = lax.axis_index("clus")
     t = lax.axis_index("trip")
@@ -119,6 +132,27 @@
     sib = (c, t, 1 - m)
     first = m == 0
 
+    fetch_eig = pltpu.make_async_copy(eig_ref.at[pl.ds(m * half, half)], elin, l_sem.at[0])
+    fetch_force = pltpu.make_async_copy(force_ref, lin, l_sem.at[1])
+    fetches = []
+    small = (
+        (table_hbm, table_ref),
+        (angle_hbm, angle_ref),
+        (freq_hbm, freq_ref),
+        (occ_hbm, occ_ref),
+        (send_rows_hbm, send_rows_ref),
+        (irr_hbm, irr_ref),
+        (mult_hbm, mult_ref),
+        (drive_hbm, drive_ref),
+        (bound_hbm, bound_ref),
+    )
+    for index, (src, dst) in enumerate(small):
+        copy = pltpu.make_async_copy(src, dst, l_sem.at[2 + index])
+        copy.start()
+        fetches.append(copy)
+    fetch_force.start()
+    fetch_eig.start()
+
     peers = []
     for dt in range(n_trip):
         for dc in range(n_clus):
@@ -136,6 +170,7 @@
         for dk in range(2):
             across.append((clus_at(axis, 1), tz if dk else t, 1 - m))
     across.append((c, tz, 1 - m))
+    across.append((c + step[0] + step[1], t, 1 - m))
 
     barrier = pltpu.get_barrier_semaphore()
     for dt, dc in peers:
@@ -143,20 +178,11 @@
     for device in across:
         pl.semaphore_signal(barrier, inc=1, device_id=device, device_id_type=MESH)
 
+    for copy in fetches:
+        copy.wait()
     asked[...] = jnp.zeros_like(asked)
     for j in range(3):
         asked[j : j + 1, :] = jnp.full((1, LANES), table_ref[c, j].astype(f32))
-
-    whole = half // 16 * 16
-    edge = flat // LANES * LANES
-    for r in range(cl):
-        at = r * rp
-        if edge < wide:
-            own[at : at + rp, edge:wide] = jnp.zeros((rp, wide - edge), bf16)
-        own[at : at + whole, :flat] = force_ref[r, :whole, :]
-        rest = force_ref[r, whole:, :].astype(f32)
-        under = jnp.zeros((rp - half, flat), f32)
-        own[at + whole : at + rp, :flat] = jnp.concatenate([rest, under], axis=0).astype(bf16)
 
     angles = angle_ref[...].astype(f32)
     here = k * n_clus + c
@@ -164,15 +190,32 @@
     tails[here, 0:cl, 0 : angles.shape[1]] = jnp.cos(angles).astype(bf16).astype(f32)
     tails[here, cl : 2 * cl, 0 : angles.shape[1]] = jnp.sin(angles).astype(bf16).astype(f32)
 
-    points = eig_ref.shape[0]
+    points = freq_ref.shape[0]
     ehalf[...] = jnp.zeros_like(ehalf)
-    for p in range(points):
-        both = eig_ref[p].astype(f32)
-        ehalf[p, 0:half, 0 : 2 * modes] = pick(m, [both[h * half : (h + 1) * half] for h in range(n_mode)])
     extra = jnp.where(first, freq_ref[...].astype(f32), occ_ref[...].astype(f32))
     for p in range(points):
         ehalf[p, half : half + 1, 0:modes] = extra[p : p + 1]
 
+    def relayout(lo, hi):
+        top = min(hi, flat)
+        if hi > flat:
+            edge = flat // LANES * LANES
+            own[:, edge:hi] = jnp.zeros((cl * rp, hi - edge), bf16)
+        for a in range(0, half, SUB):
+            n = min(SUB, half - a)
+            part = lin[a : a + n, :, lo:top]
+            if n < SUB:
+                part = jnp.concatenate([part, jnp.zeros((SUB - n, cl, top - lo), bf16)], axis=0)
+            own[a * cl : (a + SUB) * cl, lo:top] = part.reshape(SUB * cl, top - lo)
+
+    def components():
+        ehalf[:, 0:half, 0 : 2 * modes] = jnp.transpose(elin[...].astype(f32), (1, 0, 2))
+
+    def prepare(e):
+        relayout(rounds[e][1], rounds[e][1] + WORKERS * rounds[e][2])
+
+    fetch_force.wait()
+    prepare(0)
     pl.semaphore_wait(barrier, len(peers) + len(across))
 
     started = []
@@ -217,7 +260,7 @@
         return (ub * 2 + kk) * 2 + mm
 
     def columns(e, w):
-        _, base, width, _ = rounds[e]
+        _, base, width, _, _ = rounds[e]
         return pl.ds(pl.multiple_of(base + w * width, LANES), width)
 
     def local(e):
@@ -229,12 +272,15 @@
         return bits[axis], cu, cv, c + step[0] + step[1]
 
     def direct(e):
-        ub, cu, cv, _ = lines(e)
+        ub, cu, cv, cd = lines(e)
         dst = fbuf.at[m, c, :, local(e)]
         recv = f_recv.at[e, m, c]
         for index, mm in enumerate((m, 1 - m)):
             send(own.at[:, columns(e, worker(1 - ub, k, mm))], dst, f_send.at[e, index], recv, (cu, t, mm))
             send(own.at[:, columns(e, worker(ub, k, mm))], dst, f_send.at[e, 2 + index], recv, (cv, t, mm))
+        if rounds[e][4]:
+            for index, mm in enumerate((m, 1 - m)):
+                send(own.at[:, columns(e, worker(1 - ub, k, mm))], dst, f_send.at[e, 5 + index], recv, (cd, t, mm))
         send(own.at[:, columns(e, worker(ub, k, 1 - m))], dst, f_send.at[e, 4], recv, sib)
 
     def got(e, g, cc):
@@ -242,6 +288,8 @@
         remote(ref, ref, f_send.at[e, 0], f_recv.at[e, g, cc], sib).wait_recv()
 
     def forward(e):
+        if rounds[e][4]:
+            return
         _, cu, cv, _ = lines(e)
         for g in range(n_mode):
             got(e, g, cu)
@@ -250,20 +298,19 @@
 
     def phased(e):
         axis = rounds[e][0]
-        ub, _, cv, cd = lines(e)
+        ub, cu, cv, cd = lines(e)
         me = worker(ub, k, m)
         fbuf[m, c, :, local(e)] = own[:, columns(e, me)]
         got(e, 1 - m, c)
         for g in range(n_mode):
+            if rounds[e][4]:
+                got(e, g, cu)
             got(e, g, cv)
             got(e, g, cd)
         weights = wphase[axis]
         for g in range(n_mode):
             for a0 in range(0, rp, SUB):
-                parts = []
-                for cc in range(n_clus):
-                    for r in range(cl):
-                        parts.append(fbuf[g, cc, r * rp + a0 : r * rp + a0 + SUB, local(e)])
+                parts = [fbuf[g, cc, a0 * cl : (a0 + SUB) * cl, local(e)] for cc in range(n_clus)]
                 out = jnp.dot(weights, jnp.concatenate(parts, axis=0), preferred_element_type=f32).astype(bf16)
                 for q in range(4):
                     for i in range(2):
@@ -281,7 +328,7 @@
         gin[:, columns(e, me)] = gout[0, m, :, local(e)]
 
     def gather(e):
-        axis, base, width, _ = rounds[e]
+        axis, base, width, _, _ = rounds[e]
         ub = bits[axis]
         for du in range(2):
             for dk in range(2):
@@ -335,13 +382,13 @@
         turned = jnp.transpose(stack)[:SUB].astype(bf16)
         row = lax.broadcasted_iota(jnp.int32, (LANES, LANES), 0)
         col = lax.broadcasted_iota(jnp.int32, (LANES, LANES), 1)
-        source = (col // (cl * SUB)) * 8 + lax.rem(col // SUB, cl)
+        source = (col // (cl * SUB)) * 8 + lax.rem(col, cl)
         for kk in range(2):
             for i in range(2):
                 spread = jnp.where(row == source + (kk * n_clus * 8 + i * cl), 1.0, 0.0).astype(bf16)
                 lset[kk * 2 + i] = jnp.dot(turned, spread, preferred_element_type=f32)
         same = lax.broadcasted_iota(jnp.int32, (SUB, LANES), 0) == lax.rem(
-            lax.broadcasted_iota(jnp.int32, (SUB, LANES), 1), SUB
+            lax.broadcasted_iota(jnp.int32, (SUB, LANES), 1) // cl, SUB
         )
         for axis in range(2):
             for du in range(2):
@@ -433,7 +480,7 @@
         lax.fori_loop(lo, hi, one, 0)
 
     def contract(e):
-        _, base, width, _ = rounds[e]
+        _, base, width, _, _ = rounds[e]
         lo, hi = base, base + WORKERS * width
         span = pl.ds(lo, hi - lo)
         ref = gsib.at[:, span]
@@ -455,8 +502,12 @@
     total = len(rounds)
 
     direct(0)
-    if total > 1:
-        direct(1)
+    for e in range(1, total):
+        prepare(e)
+        if e < 2:
+            direct(e)
+    fetch_eig.wait()
+    components()
     forward(0)
     if total > 2:
         direct(2)
@@ -536,7 +587,7 @@
     for copy in copies:
         copy.wait()
 
-    nq = gamma_ref.shape[0]
+    nq = out_ref.shape[1]
     for q in range(nq):
         name = (t * nq + q).astype(f32)
 
@@ -550,8 +601,8 @@
         else:
             total = lax.fori_loop(0, len(peers), lambda i, acc: acc + kept(inbox[i]), total)
         gamma = total[0:1] + bound_ref[q : q + 1, :]
-        gamma_ref[q : q + 1, :] = gamma
-        dev_ref[q : q + 1, :] = (drive_ref[q : q + 1, :] + total[1:2]) / gamma
+        out_ref[0, q : q + 1, :] = gamma
+        out_ref[1, q : q + 1, :] = (drive_ref[q : q + 1, :] + total[1:2]) / gamma
 
 
 def body(
@@ -570,26 +621,42 @@
     n_clus, n_trip, n_mode = (lax.axis_size(name) for name in ("clus", "trip", "mode"))
     cl, half, flat = force_third.shape
     points, modes, _ = eigenvectors.shape
+    force_third = jnp.transpose(force_third, (1, 0, 2))
+    eigenvectors = jnp.transpose(eigenvectors, (1, 0, 2))
     slot = send_rows.shape[1] // n_trip
     rounds = plan(flat)
     count = len(rounds)
     rp = up(half, 16)
     ep = up(modes + 1, 16)
-    share = sum(width for _, _, width, _ in rounds)
+    share = sum(width for _, _, width, _, _ in rounds)
     npad = share * WORKERS
     elanes = up(2 * modes, LANES)
     n_peers = n_clus * n_trip - 1
     vmem = pl.BlockSpec(memory_space=pltpu.VMEM)
-    smem = pl.BlockSpec(memory_space=pltpu.SMEM)
-    out = jax.ShapeDtypeStruct(boundary.shape, f32)
+    small = (
+        (phase_angle, pltpu.VMEM),
+        (frequencies, pltpu.VMEM),
+        (deviation, pltpu.VMEM),
+        (send_rows, pltpu.SMEM),
+        (trip_table, pltpu.SMEM),
+        (irreducible, pltpu.SMEM),
+        (multiplicity, pltpu.SMEM),
+        (drive_term, pltpu.VMEM),
+        (boundary, pltpu.VMEM),
+    )
+    anywhere = pl.BlockSpec(memory_space=pl.ANY)
+    out = jax.ShapeDtypeStruct((2,) + boundary.shape, f32)
     dma = pltpu.SemaphoreType.DMA
-    return tuple(
+    packed = (
         pl.pallas_call(
             functools.partial(kernel, (n_clus, n_trip, n_mode, modes, half, rp, cl, slot, rounds)),
-            out_shape=(out, out),
-            in_specs=[vmem, vmem, vmem, vmem, vmem, smem, smem, smem, smem, vmem, vmem],
-            out_specs=(vmem, vmem),
-            scratch_shapes=[
+            out_shape=out,
+            in_specs=[anywhere] * (2 + len(small)),
+            out_specs=vmem,
+            scratch_shapes=[space(value.shape, value.dtype) for value, space in small]
+            + [
+                pltpu.VMEM((half, cl, flat), bf16),
+                pltpu.VMEM((half, points, 2 * modes), bf16),
                 pltpu.VMEM((cl * rp, npad), bf16),
                 pltpu.VMEM((n_mode, n_clus, cl * rp, share), bf16),
                 pltpu.VMEM((4, n_mode, 2 * rp, share), bf16),
@@ -633,24 +700,14 @@
                 dma,
                 dma((n_peers,)),
                 dma((n_peers,)),
+                dma((2 + len(small),)),
             ],
             compiler_params=pltpu.CompilerParams(
-                collective_id=0, has_side_effects=True, vmem_limit_bytes=48 * 1024 * 1024
+                collective_id=0, has_side_effects=True, vmem_limit_bytes=VMEM_BYTES
             ),
-        )(
-            force_third,
-            phase_angle,
-            eigenvectors,
-            frequencies,
-            deviation,
-            send_rows,
-            trip_table,
-            irreducible,
-            multiplicity,
-            drive_term,
-            boundary,
-        )
+        )(force_third, eigenvectors, *(value for value, _ in small))
     )
+    return packed[0], packed[1]
 
 
 def solution(mesh):

time: 50.3 us -> 47.1 us (0.936)
  local copies, waits for them, and re-layouts: 4.37 us -> 1.18 us
    unnamed x22 -> x0, local copies, waits for them, and re-layouts: 4.37 us -> none
    squeeze x0 -> x1, local copies, waits for them, and re-layouts: none -> 1.18 us  [body(): return (packed[0], packed[1])]
where the time goes in v2:
time: 47.1 us; the launch traced here: 46.9 us
  Pallas kernels  45.1 us (96%)
  local copies, waits for them, and re-layouts  1.18 us (3%)
  between operations  0.64 us (1%)
    pallas_call x1, Pallas kernels, body(): pl.pallas_call(functools.partial(kernel, (n_clus, n_trip, n_mode, modes,...  45.1 us
    squeeze x1, local copies, waits for them, and re-layouts, body(): return (packed[0], packed[1])  1.18 us

profile of v2, /device:TPU:0, one launch (start us, length us, event | category | flops | bytes accessed | tf_op | source)
XLA Modules:
  0.0 46.9 jit_solution(13309859021891898101)
XLA Ops:
  0.6 45.1 %shard_map.122 = f32[2,1,45]{2,1,0:T(1,128)} custom-call(bf16[45,2,8100]{2,1,0:T(2,128)(2,1)} %bitcast.6, bf16[90,8,180]{2,1,0:T(8,128)(2,1)} %bitcast.7, bf16[2,4]{1,0:T(2,128)(2,1)} %angle_hbm.1, bf16[8,90]{1,0:T(8,128)(2,1)} %freq_hbm.1, bf16[8,90]{1,0:T(8,128)(2,1)} %occ_hbm.1, s32[1,32]{1,0:T(1,128)} %send_rows_hbm.1, s32[4,3]{1,0:T(4,128)} %table_hbm.1, ...), custom_call_target="tpu_custom_call" | custom-call | tf_op jit(solution)/shard_map/pallas_call | solution.py:651
  45.8 1.2 %slice_bitcast_fusion = (f32[1,45]{1,0:T(1,128)}, f32[1,45]{1,0:T(1,128)}) fusion(f32[2,1,45]{2,1,0:T(1,128)} %shard_map.122), kind=kLoop, calls=%fused_computation | loop fusion | bytes 720 | tf_op jit(solution)/shard_map/squeeze | solution.py:710
